TPU v7x, 32 devices: a whole 2x2x4 slice. The times are simulated.
32 devices in a mesh: gx: 4 (over x, core), gy: 8 (over z, y).
Axes of the slice: x: 2, y: 2, z: 4, core: 2. Of those that a mesh axis runs over, the one named last changes fastest.
Arguments:
- velocity: float32 [16, 384, 8192], P(None, 'gy', 'gx'), may hold values from -8 to 8
- blend_left: float32 [128, 10], replicated, may hold values from -2 to 2
- blend_right: float32 [128, 10], replicated, may hold values from -2 to 2
- injection: float32 [16], replicated, may hold values from 0.5 to 2
Outputs:
- dudx: float32 [16, 384, 8192], P(None, 'gy', 'gx')
- rhs: float32 [16, 384, 8192], P(None, 'gy', 'gx')
All inputs are finite; a program needn't handle non-finite values.
Results may differ from a plain program's by a relative error of at most 0.000086.
Values sent between devices are 32-bit elements; how exact they have to be, the bound alone decides.
A program may use at most 128 MiB of HBM per device.

v0:
```python
import math

import jax
import jax.numpy as jnp
from jax import lax
from jax.sharding import PartitionSpec as P

DEND = 10


TWO_PI = 2.0 * math.pi
ALPHA = 36.0
ORDER = 36
HIGH = lax.Precision.HIGHEST


def rotation(expo, modulus):
    angle = (expo % modulus).astype(jnp.float32) * (TWO_PI / modulus)
    return (jnp.cos(angle), -jnp.sin(angle))


def tables(rows_p, cols_q):
    modulus = rows_p * cols_q
    index_p = jnp.arange(rows_p, dtype=jnp.int32)
    index_q = jnp.arange(cols_q, dtype=jnp.int32)
    outer_p = rotation(cols_q * index_p[:, None] * index_p[None, :], modulus)
    outer_q = rotation(rows_p * index_q[:, None] * index_q[None, :], modulus)
    twiddle = rotation(index_p[:, None] * index_q[None, :], modulus)
    freq = index_p[:, None] + rows_p * index_q[None, :]
    half = modulus // 2
    signed = jnp.where(freq < half, freq, freq - modulus).astype(jnp.float32)
    ratio = jnp.abs(signed) / half
    value = TWO_PI / modulus * signed * jnp.exp(-ALPHA * ratio**ORDER)
    factor = jnp.where(freq == half, jnp.zeros_like(value), value)
    return (outer_p, outer_q, twiddle, factor)


def mix(form, left, right):
    return jnp.einsum(form, left, right, precision=HIGH)


def continuation(left, right, blend_left, blend_right):
    return jnp.dot(left, blend_left.T, precision=HIGH) + jnp.dot(
        right, blend_right.T, precision=HIGH
    )


def derivative_lines(full, cont):
    own = full.shape[0]
    cols_q = cont.shape[1]
    rows_p = full.shape[1] // cols_q + 1
    (fp_re, fp_im), (fq_re, fq_im), (tw_re, tw_im), factor = tables(rows_p, cols_q)
    inner = full.reshape(own, rows_p - 1, cols_q)
    a_re = (
        mix("kj,ljq->lkq", fp_re[:, : rows_p - 1], inner)
        + fp_re[None, :, rows_p - 1 :] * cont[:, None, :]
    )
    a_im = (
        mix("kj,ljq->lkq", fp_im[:, : rows_p - 1], inner)
        + fp_im[None, :, rows_p - 1 :] * cont[:, None, :]
    )
    b_re = a_re * tw_re - a_im * tw_im
    b_im = a_re * tw_im + a_im * tw_re
    e_re = mix("lkq,qm->lkm", b_re, fq_re) - mix("lkq,qm->lkm", b_im, fq_im)
    e_im = mix("lkq,qm->lkm", b_re, fq_im) + mix("lkq,qm->lkm", b_im, fq_re)
    d_re = -factor * e_im
    d_im = factor * e_re
    f_re = mix("lkm,mq->lkq", d_re, fq_re) + mix("lkm,mq->lkq", d_im, fq_im)
    f_im = mix("lkm,mq->lkq", d_im, fq_re) - mix("lkm,mq->lkq", d_re, fq_im)
    g_re = f_re * tw_re + f_im * tw_im
    g_im = f_im * tw_re - f_re * tw_im
    deriv = mix("jk,lkq->ljq", fp_re[: rows_p - 1], g_re) + mix(
        "jk,lkq->ljq", fp_im[: rows_p - 1], g_im
    )
    return (deriv / (rows_p * cols_q)).reshape(own, full.shape[1])


def per_device(velocity, blend_left, blend_right, injection):
    planes, rows, width = velocity.shape
    groups = lax.axis_size("gx")
    total_lines = planes * rows
    lines = velocity.reshape(total_lines, width)
    full = lax.all_to_all(lines, "gx", split_axis=0, concat_axis=1, tiled=True)
    length = full.shape[1]
    cont = continuation(full[:, :DEND], full[:, length - DEND :], blend_left, blend_right)
    deriv = derivative_lines(full, cont)
    local_energy = jnp.sum(velocity * velocity, axis=(1, 2))
    total_energy = lax.psum(local_energy, ("gx", "gy"))
    energy = total_energy / (width * groups * rows * lax.axis_size("gy"))
    forcing = injection / energy
    dudx = lax.all_to_all(deriv, "gx", split_axis=1, concat_axis=0, tiled=True).reshape(
        planes, rows, width
    )
    rhs = -velocity * dudx + forcing[:, None, None] * velocity
    return (dudx, rhs)


def solution(mesh):
    placed = (P(None, "gy", "gx"), P(), P(), P())
    return jax.shard_map(
        per_device,
        mesh=mesh,
        in_specs=placed,
        out_specs=(P(None, "gy", "gx"), P(None, "gy", "gx")),
        check_vma=False,
    )
```

profile of v0, /device:TPU:0, one launch (start us, length us, event | category | flops | bytes accessed | tf_op | source)
XLA Modules:
  0.0 396.7 jit_solution(4331970692347266028)
XLA Ops:
  0.6 0.0 copy-start
  0.6 5.3 %all-to-all-start = ((f32[4,192,2048]{2,1,0:T(8,128)}), f32[4,192,2048]{2,1,0:T(8,128)}, u32[]{:S(2)}, u32[]{:S(2)}) async-start(f32[4,192,2048]{2,1,0:T(8,128)} %bitcast.65), calls=%async_computation | async-start | bytes 12582912 | tf_op jit(solution)/shard_map/all_to_all | solution.py:83
  6.0 0.2 sine_negate_fusion.5
  6.1 0.2 sine_negate_fusion.6
  6.4 70.9 %all-to-all-done = f32[4,192,2048]{2,1,0:T(8,128)} async-done(((f32[4,192,2048]{2,1,0:T(8,128)}), f32[4,192,2048]{2,1,0:T(8,128)}, u32[]{:S(2)}, u32[]{:S(2)}) %all-to-all-start) | async-done | bytes 6291488 | tf_op jit(solution)/shard_map/all_to_all | solution.py:83
  77.3 9.5 %copy.30 = f32[192,4,2048]{2,1,0:T(4,128)} copy(f32[192,4,2048]{2,0,1:T(8,128)} %bitcast.2) | data formatting | bytes 12582912 | tf_op jit(solution)/shard_map/all_to_all | solution.py:83
  86.8 8.2 %reshape.130 = f32[192,64,128]{2,1,0:T(8,128)} reshape(f32[192,4,2048]{2,1,0:T(4,128)} %copy.30) | data formatting | bytes 12582912 | tf_op jit(solution)/shard_map/reshape | solution.py:53
  95.0 0.0 slice-start
  95.0 0.0 slice-start.1
  95.0 3.4 copy.47
  98.4 0.6 slice-done
  99.0 0.7 slice-done.1
  99.7 0.0 copy-start.3
  99.7 8.0 %fusion.65 = f32[65,192,128]{2,0,1:T(8,128)} fusion(f32[192,64,128]{2,1,0:T(8,128)S(1)} %bitcast.67, f32[65,65]{0,1:T(8,128)S(1)} %get-tuple-element.6), kind=kOutput, calls=%fused_computation.82 | convolution fusion | flops 1226833920 | bytes 12713984 | tf_op jit(solution)/shard_map/kj,ljq->lkq/dot_general | solution.py:39
  107.7 0.0 copy-done
  107.7 0.2 fusion.27
  107.9 0.0 copy-done.3
  107.9 0.3 convolution_add_fusion
  108.2 10.9 %multiply_subtract_fusion = (f32[192,65,128]{2,1,0:T(8,128)S(1)}, f32[192,65,128]{2,1,0:T(8,128)S(1)}) fusion(f32[65,192,128]{2,0,1:T(8,128)} %fusion.65, f32[65,128]{1,0:T(8,128)S(1)} %get-tuple-element.10, f32[65]{0:T(128)S(1)} %get-tuple-element.8, f32[65,128]{1,0:T(8,128)S(1)} %get-tuple-element.11, f32[192,128]{1,0:T(8,128)S(1)} %convolution_add_fusion, ...), kind=kOutput, calls=%fused_computation.13 | convolution fusion | flops 1242808320 | bytes 25666560 | tf_op jit(solution)/shard_map/kj,ljq->lkq/dot_general | solution.py:39
  119.1 0.0 copy-start.2
  119.1 5.7 %fusion.8 = f32[192,65,128]{2,0,1:T(8,128)S(1)} fusion(f32[192,65,128]{2,1,0:T(8,128)S(1)} %get-tuple-element.3, s32[128]{0:T(128)S(1)} %iota_multiply_fusion.1), kind=kOutput, calls=%fused_computation.19 | convolution fusion | flops 2453831680 | bytes 12780032 | tf_op jit(solution)/shard_map/lkq,qm->lkm/dot_general | solution.py:39
  124.8 8.0 %fusion.10 = f32[192,65,128]{2,0,1:T(8,128)} fusion(f32[192,65,128]{2,1,0:T(8,128)S(1)} %get-tuple-element.3, s32[128]{0:T(128)S(1)} %iota_multiply_fusion.1), kind=kOutput, calls=%fused_computation.21 | convolution fusion | flops 2453815296 | bytes 12780032 | tf_op jit(solution)/shard_map/lkq,qm->lkm/dot_general | solution.py:39
  132.9 0.0 copy-done.2
  132.9 5.7 %subtract_multiply_fusion = f32[192,65,128]{2,0,1:T(8,128)S(1)} fusion(f32[192,65,128]{2,0,1:T(8,128)S(1)} %fusion.8, f32[65,128]{1,0:T(8,128)S(1)} %get-tuple-element.5, f32[192,65,128]{2,1,0:T(8,128)S(1)} %get-tuple-element.2, s32[128]{0:T(128)S(1)} %iota_multiply_fusion.1), kind=kOutput, calls=%fused_computation.14 | convolution fusion | flops 2457010176 | bytes 19203072 | tf_op jit(solution)/shard_map/lkq,qm->lkm/dot_general | solution.py:39
  138.6 0.0 slice-start.2
  138.6 5.8 %fusion.31 = f32[192,65,128]{2,0,1:T(8,128)S(1)} fusion(f32[192,65,128]{2,0,1:T(8,128)S(1)} %subtract_multiply_fusion, s32[128]{0:T(128)S(1)} %iota_multiply_fusion.1), kind=kOutput, calls=%fused_computation.39 | convolution fusion | flops 2453815296 | bytes 12780032 | tf_op jit(solution)/shard_map/lkm,mq->lkq/dot_general | solution.py:39
  144.4 0.0 slice-start.3
  144.4 6.0 %fusion.39 = f32[192,65,128]{2,0,1:T(8,128)S(1)} fusion(f32[192,65,128]{2,0,1:T(8,128)S(1)} %subtract_multiply_fusion, s32[128]{0:T(128)S(1)} %iota_multiply_fusion.1), kind=kOutput, calls=%fused_computation.47 | convolution fusion | flops 2453831680 | bytes 12780032 | tf_op jit(solution)/shard_map/lkm,mq->lkq/dot_general | solution.py:39
  150.4 0.0 slice-done.2
  150.4 0.0 slice-done.3
  150.4 7.9 %add_multiply_fusion = f32[192,65,128]{2,0,1:T(8,128)S(1)} fusion(f32[192,65,128]{2,0,1:T(8,128)} %fusion.10, f32[65,128]{1,0:T(8,128)S(1)} %get-tuple-element.4, f32[192,65,128]{2,1,0:T(8,128)S(1)} %bitcast.69, s32[128]{0:T(128)S(1)} %iota_multiply_fusion.1), kind=kOutput, calls=%fused_computation.15 | convolution fusion | flops 2457026560 | bytes 19203072 | tf_op jit(solution)/shard_map/lkq,qm->lkm/dot_general | solution.py:39
  158.4 7.6 %fusion.37 = f32[192,65,128]{2,0,1:T(8,128)} fusion(f32[192,65,128]{2,0,1:T(8,128)S(1)} %add_multiply_fusion, s32[128]{0:T(128)S(1)} %iota_multiply_fusion.1), kind=kOutput, calls=%fused_computation.45 | convolution fusion | flops 2453831680 | bytes 12780032 | tf_op jit(solution)/shard_map/lkm,mq->lkq/dot_general | solution.py:39
  166.0 7.6 %fusion.34 = f32[192,65,128]{2,0,1:T(8,128)} fusion(f32[192,65,128]{2,0,1:T(8,128)S(1)} %add_multiply_fusion, s32[128]{0:T(128)S(1)} %iota_multiply_fusion.1), kind=kOutput, calls=%fused_computation.42 | convolution fusion | flops 2453815296 | bytes 12780032 | tf_op jit(solution)/shard_map/lkm,mq->lkq/dot_general | solution.py:39
  173.7 38.4 %fusion = f32[192,128,64]{1,2,0:T(8,128)} fusion(f32[65,128]{1,0:T(8,128)S(1)} %get-tuple-element.10, f32[65,128]{1,0:T(8,128)S(1)} %get-tuple-element.11, f32[192,65,128]{2,0,1:T(8,128)S(1)} %fusion.39, f32[192,65,128]{2,0,1:T(8,128)} %fusion.34, f32[192,65,128]{2,0,1:T(8,128)} %fusion.37, f32[192,65,128]{2,0,1:T(8,128)S(1)} %fusion.31, ...), kind=kOutput, calls=%fused_computation.4 | convolution fusion | flops 1234821120 | bytes 31933956 | tf_op jit(solution)/shard_map/jk,lkq->ljq/dot_general | solution.py:39
  212.1 40.5 %multiply_bitcast_fusion = f32[192,64,128]{2,1,0:T(8,128)} fusion(f32[192,128,64]{1,2,0:T(8,128)} %fusion, f32[65,128]{1,0:T(8,128)S(1)} %get-tuple-element.10, f32[65,128]{1,0:T(8,128)S(1)} %get-tuple-element.11, f32[192,65,128]{2,0,1:T(8,128)S(1)} %fusion.39, f32[192,65,128]{2,0,1:T(8,128)} %fusion.34, f32[192,65,128]{2,0,1:T(8,128)} %fusion.37, ...), kind=kOutput, calls=%fused_computation.18 | convolution fusion | flops 1237966848 | bytes 38225412 | tf_op jit(solution)/shard_map/jk,lkq->ljq/dot_general | solution.py:39
  252.6 7.5 %all_to_all.30 = f32[192,4,2048]{2,1,0:T(4,128)} reshape(f32[192,64,128]{2,1,0:T(8,128)} %multiply_bitcast_fusion) | data formatting | bytes 12582912 | tf_op jit(solution)/shard_map/all_to_all | solution.py:91
  260.1 9.1 %copy.42 = f32[192,4,2048]{2,0,1:T(8,128)} copy(f32[192,4,2048]{2,1,0:T(4,128)} %all_to_all.30) | data formatting | bytes 12582912 | tf_op jit(solution)/shard_map/all_to_all | solution.py:91
  269.3 0.0 copy-start.4
  269.3 5.4 %all-to-all-start.1 = ((f32[192,4,2048]{2,0,1:T(8,128)}), f32[192,4,2048]{2,0,1:T(8,128)}, u32[]{:S(2)}, u32[]{:S(2)}) async-start(f32[192,4,2048]{2,0,1:T(8,128)} %copy.42), calls=%async_computation.1 | async-start | bytes 12582912 | tf_op jit(solution)/shard_map/all_to_all | solution.py:91
  274.7 3.4 multiply_reduce_fusion
  278.0 102.5 %psum.7 = f32[16]{0:T(128)S(1)} all-reduce(f32[16]{0:T(128)S(1)} %multiply_reduce_fusion), channel_id=1, replica_groups=mesh['gx'=4,'gy'=8] {'gx','gy'}, use_global_device_ids=true, to_apply=%region_1.2 | all-reduce | flops 16 | bytes 128 | tf_op jit(solution)/shard_map/psum | solution.py:88
  380.5 0.0 copy-done.4
  380.5 0.0 all-to-all-done.1
  380.5 0.0 copy-start.1
  380.5 9.6 %multiply_add_fusion.1 = f32[16,48,2048]{2,1,0:T(8,128)} fusion(f32[16,48,2048]{2,1,0:T(8,128)} %param.4, f32[16,48,2048]{2,1,0:T(8,128)} %bitcast.14, f32[16]{0:T(128)S(1)} %multiply_divide_fusion), kind=kLoop, calls=%fused_computation.16 | loop fusion | flops 6291456 | bytes 18874432 | tf_op jit(solution)/shard_map/add | solution.py:94
  390.2 6.3 %copy.97 = f32[16,48,2048]{2,1,0:T(8,128)} copy(f32[16,48,2048]{2,1,0:T(8,128)} %bitcast.14) | data formatting | bytes 12582912
  396.5 0.0 copy-done.1
  (7 shorter events, 0.1 us)
Async XLA Ops:
  0.6 107.1 %copy-start = (f32[128,10]{0,1:T(8,128)S(1)}, f32[128,10]{0,1:T(8,128)}, u32[]{:S(2)}) copy-start(f32[128,10]{0,1:T(8,128)} %param.5) | copy-start | bytes 15364
  0.6 76.6 %all-to-all-start = ((f32[4,192,2048]{2,1,0:T(8,128)}), f32[4,192,2048]{2,1,0:T(8,128)}, u32[]{:S(2)}, u32[]{:S(2)}) async-start(f32[4,192,2048]{2,1,0:T(8,128)} %bitcast.65), calls=%async_computation | async-start | bytes 12582912 | tf_op jit(solution)/shard_map/all_to_all | solution.py:83
  95.0 4.0 %slice-start = ((s8[6291456]{0:T(1024)(128)(4,1)}), s8[4194304]{0:T(1024)(128)(4,1)S(1)}, s32[]{:S(2)}) async-start(s8[6291456]{0:T(1024)(128)(4,1)} %bitcast.66), calls=%async_computation.2 | async-start | bytes 8388608
  95.0 4.7 %slice-start.1 = ((s8[6291456]{0:T(1024)(128)(4,1)}), s8[2097152]{0:T(1024)(128)(4,1)S(1)}, s32[]{:S(2)}) async-start(s8[6291456]{0:T(1024)(128)(4,1)} %bitcast.66), calls=%async_computation.3 | async-start | bytes 4194304
  99.7 8.2 %copy-start.3 = (f32[128,10]{0,1:T(8,128)S(1)}, f32[128,10]{0,1:T(8,128)}, u32[]{:S(2)}) copy-start(f32[128,10]{0,1:T(8,128)} %param.6) | copy-start | bytes 15364
  119.1 13.8 %copy-start.2 = (f32[192,65,128]{2,1,0:T(8,128)}, f32[192,65,128]{2,1,0:T(8,128)S(1)}, u32[]{:S(2)}) copy-start(f32[192,65,128]{2,1,0:T(8,128)S(1)} %get-tuple-element.2) | copy-start | bytes 19169284
  138.6 11.8 %slice-start.2 = ((s8[7077888]{0:T(1024)(128)(4,1)}), s8[4194304]{0:T(1024)(128)(4,1)S(1)}, s32[]{:S(2)}) async-start(s8[7077888]{0:T(1024)(128)(4,1)} %bitcast.68), calls=%async_computation.4 | async-start | bytes 8388608
  144.4 6.1 %slice-start.3 = ((s8[7077888]{0:T(1024)(128)(4,1)}), s8[2883584]{0:T(1024)(128)(4,1)S(1)}, s32[]{:S(2)}) async-start(s8[7077888]{0:T(1024)(128)(4,1)} %bitcast.68), calls=%async_computation.5 | async-start | bytes 5767168
  269.3 111.3 %copy-start.4 = (f32[16]{0:T(128)S(1)}, f32[16]{0:T(128)}, u32[]{:S(2)}) copy-start(f32[16]{0:T(128)} %param.7) | copy-start | bytes 196
  269.3 111.3 %all-to-all-start.1 = ((f32[192,4,2048]{2,0,1:T(8,128)}), f32[192,4,2048]{2,0,1:T(8,128)}, u32[]{:S(2)}, u32[]{:S(2)}) async-start(f32[192,4,2048]{2,0,1:T(8,128)} %copy.42), calls=%async_computation.1 | async-start | bytes 12582912 | tf_op jit(solution)/shard_map/all_to_all | solution.py:91
  380.5 15.9 %copy-start.1 = (f32[128,10]{0,1:T(8,128)S(1)}, f32[128,10]{0,1:T(8,128)}, u32[]{:S(2)}) copy-start(f32[128,10]{0,1:T(8,128)} %param.5) | copy-start | bytes 15364
where the time goes:
time: 404 us; the launch traced here: 397 us
  matrix products  153 us (38%)
  blocking collectives  102 us (25%)
  waiting for transfers between devices  70.9 us (18%)
  local copies, waits for them, and re-layouts  45.5 us (11%)
  other arithmetic  13.4 us (3%)
  starting transfers between devices  10.7 us (3%)
    dot_general x12, matrix products, mix(): return jnp.einsum(form, left, right, precision=HIGH)  152 us
    psum x1, blocking collectives, per_device(): total_energy = lax.psum(local_energy, ('gx', 'gy'))  102 us
    all_to_all x1, waiting for transfers between devices, per_device(): full = lax.all_to_all(lines, 'gx', split_axis=0, concat_axis=1, tiled=True)  70.9 us
    all_to_all x2, local copies, waits for them, and re-layouts, per_device(): lax.all_to_all(deriv, 'gx', split_axis=1, concat_axis=0, tiled=True)  16.7 us
    all_to_all x2, local copies, waits for them, and re-layouts, per_device(): full = lax.all_to_all(lines, 'gx', split_axis=0, concat_axis=1, tiled=True)  12.9 us
    add x1, other arithmetic, per_device(): rhs = -velocity * dudx + forcing[:, None, None] * velocity  9.62 us
    reshape x1, local copies, waits for them, and re-layouts, derivative_lines(): inner = full.reshape(own, rows_p - 1, cols_q)  8.24 us
  transfers between devices with their start and end apart: 2, of which 1 were waited for; matrix products, arithmetic and copies ran while one was open for 1% of the time, Pallas kernels for 0%

commit v1 on v0

v1 whole, which is shorter than its diff:
```python
import functools

import jax
import jax.numpy as jnp
import numpy as np
from jax import lax
from jax.experimental import pallas as pl
from jax.experimental.pallas import tpu as pltpu
from jax.sharding import PartitionSpec as P

ALPHA = 36.0
ORDER = 36
BLOCK = 256
PACK = 16
HIGH = lax.Precision.HIGHEST


def taps(period):
    freq = np.arange(period)
    half = period // 2
    signed = np.where(freq < half, freq, freq - period).astype(np.float64)
    factor = 2.0 * np.pi / period * signed * np.exp(-ALPHA * (np.abs(signed) / half) ** ORDER)
    factor[half] = 0.0
    return np.fft.ifft(1j * factor).real


def toeplitz(period, reach):
    kernel = taps(period)
    source = np.arange(BLOCK + 2 * reach)[:, None] - reach
    target = np.arange(BLOCK)[None, :]
    table = kernel[(target - source) % period]
    high = table.astype(np.float32).astype(jnp.bfloat16)
    low = (table - high.astype(np.float64)).astype(np.float32).astype(jnp.bfloat16)
    return high, low


def exchange_kernel(
    nx, ny, v_ref, bl_ref, br_ref, left_ref, right_ref, total_ref,
    vbuf, xbuf, ybuf, part, ends, blend, cont,
    load_sem, xsend, xrecv, ysend, yrecv, hsend, hrecv, esend, erecv, csem,
):
    planes, rows, width = v_ref.shape
    reach = left_ref.shape[2]
    depth = bl_ref.shape[1]
    gx = lax.axis_index("gx")
    gy = lax.axis_index("gy")
    first = gx == 0
    last = gx == nx - 1

    def load(p):
        return pltpu.make_async_copy(v_ref.at[p], vbuf.at[p], load_sem.at[p])

    def start_load(p, carry):
        load(p).start()
        return carry

    lax.fori_loop(0, planes, start_load, 0)

    barrier = pltpu.get_barrier_semaphore()
    for d in range(1, nx):
        pl.semaphore_signal(barrier, inc=1, device_id={"gx": lax.rem(gx + d, nx)})
    for d in range(1, ny):
        pl.semaphore_signal(barrier, inc=1, device_id={"gy": lax.rem(gy + d, ny)})
    pl.semaphore_wait(barrier, nx + ny - 2)

    to_right = pltpu.make_async_remote_copy(
        src_ref=v_ref.at[:, :, pl.ds(width - reach, reach)],
        dst_ref=left_ref,
        send_sem=hsend.at[0],
        recv_sem=hrecv.at[0],
        device_id={"gx": lax.rem(gx + 1, nx)},
    )
    to_left = pltpu.make_async_remote_copy(
        src_ref=v_ref.at[:, :, pl.ds(0, reach)],
        dst_ref=right_ref,
        send_sem=hsend.at[1],
        recv_sem=hrecv.at[1],
        device_id={"gx": lax.rem(gx + nx - 1, nx)},
    )

    @pl.when(jnp.logical_not(last))
    def _():
        to_right.start()

    @pl.when(jnp.logical_not(first))
    def _():
        to_left.start()

    def plane_sum(p, carry):
        load(p).wait()
        x = vbuf[p]
        s = jnp.sum((x * x).reshape(rows // 8, 8, width), axis=0)
        acc = s[:, 0:128]
        for c in range(1, width // 128):
            acc = acc + s[:, c * 128 : (c + 1) * 128]
        part[pl.ds(p, 1), :] = jnp.sum(acc, axis=0, keepdims=True)
        return carry

    lax.fori_loop(0, planes, plane_sum, 0)

    xcopies = []
    for d in range(1, nx):
        copy = pltpu.make_async_remote_copy(
            src_ref=part,
            dst_ref=xbuf.at[d],
            send_sem=xsend.at[d],
            recv_sem=xrecv.at[d],
            device_id={"gx": lax.rem(gx + d, nx)},
        )
        copy.start()
        xcopies.append(copy)

    sel_row = lax.broadcasted_iota(jnp.int32, (PACK, reach), 0)
    sel_col = lax.broadcasted_iota(jnp.int32, (PACK, reach), 1)

    def pack(lane, offset):
        pick = jnp.where((sel_row < depth) & (sel_col == sel_row + offset), 1.0, 0.0)
        tile = vbuf[:, :, lane : lane + reach].reshape(planes * rows, reach)
        return lax.dot_general(
            pick.astype(jnp.float32), tile, (((1,), (1,)), ((), ())), precision=HIGH
        )

    ends_out = pltpu.make_async_remote_copy(
        src_ref=ends.at[0], dst_ref=ends.at[0], send_sem=esend.at[0],
        recv_sem=erecv.at[0], device_id={"gx": nx - 1},
    )
    ends_back = pltpu.make_async_remote_copy(
        src_ref=ends.at[1], dst_ref=ends.at[1], send_sem=esend.at[1],
        recv_sem=erecv.at[1], device_id={"gx": 0},
    )

    @pl.when(first)
    def _():
        ends[0] = pack(0, 0)
        ends_out.start()

    @pl.when(last)
    def _():
        ends[1] = pack(width - reach, reach - depth)
        ends_back.start()

    for copy in xcopies:
        copy.wait()
    mine = part[...]
    for d in range(1, nx):
        mine = mine + xbuf[d]
    ybuf[0] = mine
    ycopies = []
    for d in range(1, ny):
        copy = pltpu.make_async_remote_copy(
            src_ref=ybuf.at[0],
            dst_ref=ybuf.at[d],
            send_sem=ysend.at[d],
            recv_sem=yrecv.at[d],
            device_id={"gy": lax.rem(gy + d, ny)},
        )
        copy.start()
        ycopies.append(copy)

    def continuation():
        blend[...] = jnp.zeros_like(blend)
        blend[0, :, 0:depth] = bl_ref[...]
        blend[1, :, 0:depth] = br_ref[...]
        turned = jnp.dot(blend[0], ends[0], precision=HIGH) + jnp.dot(
            blend[1], ends[1], precision=HIGH
        )
        cont[...] = jnp.transpose(turned).reshape(cont.shape)

    @pl.when(first)
    def _():
        ends_out.wait_send()
        ends_back.wait_recv()
        continuation()
        out = pltpu.make_async_copy(cont, left_ref, csem)
        out.start()
        out.wait()

    @pl.when(last)
    def _():
        ends_back.wait_send()
        ends_out.wait_recv()
        continuation()
        out = pltpu.make_async_copy(cont, right_ref, csem)
        out.start()
        out.wait()

    for copy in ycopies:
        copy.wait()
    every = ybuf[0]
    for d in range(1, ny):
        every = every + ybuf[d]
    total_ref[...] = every

    @pl.when(jnp.logical_not(last))
    def _():
        to_right.wait_send()
        to_left.wait_recv()

    @pl.when(jnp.logical_not(first))
    def _():
        to_left.wait_send()
        to_right.wait_recv()


def exchange(velocity, blend_left, blend_right, nx, ny):
    planes, rows, width = velocity.shape
    reach = blend_left.shape[0]
    halo = jax.ShapeDtypeStruct((planes, rows, reach), jnp.float32)
    dma = pltpu.SemaphoreType.DMA
    return pl.pallas_call(
        functools.partial(exchange_kernel, nx, ny),
        out_shape=(halo, halo, jax.ShapeDtypeStruct((planes, 128), jnp.float32)),
        in_specs=[
            pl.BlockSpec(memory_space=pl.ANY),
            pl.BlockSpec(memory_space=pltpu.VMEM),
            pl.BlockSpec(memory_space=pltpu.VMEM),
        ],
        out_specs=(
            pl.BlockSpec(memory_space=pl.ANY),
            pl.BlockSpec(memory_space=pl.ANY),
            pl.BlockSpec(memory_space=pltpu.VMEM),
        ),
        scratch_shapes=[
            pltpu.VMEM((planes, rows, width), jnp.float32),
            pltpu.VMEM((nx, planes, 128), jnp.float32),
            pltpu.VMEM((ny, planes, 128), jnp.float32),
            pltpu.VMEM((planes, 128), jnp.float32),
            pltpu.VMEM((2, PACK, planes * rows), jnp.float32),
            pltpu.VMEM((2, reach, PACK), jnp.float32),
            pltpu.VMEM((planes, rows, reach), jnp.float32),
            dma((planes,)),
            dma((nx,)),
            dma((nx,)),
            dma((ny,)),
            dma((ny,)),
            dma((2,)),
            dma((2,)),
            dma((2,)),
            dma((2,)),
            dma,
        ],
        compiler_params=pltpu.CompilerParams(
            collective_id=0, has_side_effects=True, vmem_limit_bytes=48 * 2**20
        ),
        name="exchange",
    )(velocity, blend_left, blend_right)


def filter_kernel(
    count, v_ref, left_ref, right_ref, high_ref, low_ref, total_ref, inj_ref,
    dudx_ref, rhs_ref, ehigh, elow,
):
    group, rows, width = v_ref.shape
    reach = left_ref.shape[2]
    lines = group * rows
    blocks = width // BLOCK

    def put(c, lane, x):
        x = x.reshape(lines, x.shape[2])
        high = x.astype(jnp.bfloat16)
        low = (x - high.astype(jnp.float32)).astype(jnp.bfloat16)
        spot = (pl.ds(c * lines, lines), pl.ds(lane, x.shape[1]))
        ehigh[spot] = high
        elow[spot] = low

    put(0, 0, left_ref[...])
    put(0, reach, v_ref[:, :, 0 : BLOCK - reach])
    for c in range(1, blocks):
        put(c, 0, v_ref[:, :, c * BLOCK - reach : (c + 1) * BLOCK - reach])
    put(blocks, 0, v_ref[:, :, width - reach :])
    put(blocks, reach, right_ref[...])

    step = pl.program_id(0)
    forcing = []
    for g in range(group):
        p = step * group + g
        energy = jnp.sum(total_ref[pl.ds(p, 1), :], axis=1, keepdims=True) / count
        forcing.append(inj_ref[p] / energy)

    chunk = min(4, blocks)
    for c0 in range(0, blocks, chunk):
        here = pl.ds(c0 * lines, chunk * lines)
        there = pl.ds((c0 + 1) * lines, chunk * lines)
        wide_high = jnp.concatenate([ehigh[here, :], ehigh[there, :]], axis=1)
        wide_low = jnp.concatenate([elow[here, :], elow[there, :]], axis=1)
        dot = functools.partial(jnp.dot, preferred_element_type=jnp.float32)
        res = dot(wide_high, high_ref[...])
        res = res + dot(wide_low, high_ref[...])
        res = res + dot(wide_high, low_ref[...])
        res = res.reshape(chunk, group, rows, BLOCK)
        for i in range(chunk):
            lane = (c0 + i) * BLOCK
            for g in range(group):
                d = res[i, g]
                dudx_ref[g, :, lane : lane + BLOCK] = d
                rhs_ref[g, :, lane : lane + BLOCK] = v_ref[g, :, lane : lane + BLOCK] * (
                    forcing[g] - d
                )


def apply_filter(velocity, left, right, total, injection, period, count):
    planes, rows, width = velocity.shape
    reach = left.shape[2]
    high, low = toeplitz(period, reach)
    group = min(4, planes)
    lines = group * rows
    blocks = width // BLOCK
    whole = jax.ShapeDtypeStruct(velocity.shape, jnp.float32)
    by_plane = lambda i: (i, 0, 0)
    fixed = lambda i: (0, 0)
    return pl.pallas_call(
        functools.partial(filter_kernel, count),
        grid=(planes // group,),
        out_shape=(whole, whole),
        in_specs=[
            pl.BlockSpec((group, rows, width), by_plane),
            pl.BlockSpec((group, rows, reach), by_plane),
            pl.BlockSpec((group, rows, reach), by_plane),
            pl.BlockSpec(high.shape, fixed),
            pl.BlockSpec(low.shape, fixed),
            pl.BlockSpec(total.shape, fixed),
            pl.BlockSpec(memory_space=pltpu.SMEM),
        ],
        out_specs=(
            pl.BlockSpec((group, rows, width), by_plane),
            pl.BlockSpec((group, rows, width), by_plane),
        ),
        scratch_shapes=[
            pltpu.VMEM(((blocks + 1) * lines, BLOCK), jnp.bfloat16),
            pltpu.VMEM(((blocks + 1) * lines, BLOCK), jnp.bfloat16),
        ],
        compiler_params=pltpu.CompilerParams(vmem_limit_bytes=56 * 2**20),
        name="filter",
    )(velocity, left, right, jnp.asarray(high), jnp.asarray(low), total, injection)


def per_device(nx, ny, velocity, blend_left, blend_right, injection):
    planes, rows, width = velocity.shape
    period = width * nx + blend_left.shape[0]
    count = width * nx * rows * ny
    left, right, total = exchange(velocity, blend_left, blend_right, nx, ny)
    return apply_filter(velocity, left, right, total, injection, period, count)


def solution(mesh):
    placed = (P(None, "gy", "gx"), P(), P(), P())
    return jax.shard_map(
        functools.partial(per_device, mesh.shape["gx"], mesh.shape["gy"]),
        mesh=mesh,
        in_specs=placed,
        out_specs=(P(None, "gy", "gx"), P(None, "gy", "gx")),
        check_vma=False,
    )
```

time: 404 us -> 32.5 us (0.08); the launches traced: 397 us -> 32.2 us
  matrix products: 153 us -> 0 us
  blocking collectives: 102 us -> 0 us
  waiting for transfers between devices: 70.9 us -> 0 us
  local copies, waits for them, and re-layouts: 45.5 us -> 3.68 us
  Pallas kernels: 0 us -> 27.9 us
  other arithmetic: 13.4 us -> 0 us
  starting transfers between devices: 10.7 us -> 0 us
    dot_general x14 -> x0, matrix products: 153 us -> none  [the longest x12 152 us: mix(): return jnp.einsum(form, left, right, precision=HIGH)]
    psum x1 -> x0, blocking collectives: 102 us -> none  [per_device(): total_energy = lax.psum(local_energy, ('gx', 'gy'))]
    all_to_all x2 -> x0, waiting for transfers between devices: 70.9 us -> none  [the longest x1 70.9 us: per_device(): full = lax.all_to_all(lines, 'gx', split_axis=0, concat_axis=1, tiled=True)]
    all_to_all x4 -> x0, local copies, waits for them, and re-layouts: 29.6 us -> none  [the longest x2 16.7 us: per_device(): lax.all_to_all(deriv, 'gx', split_axis=1, concat_axis=0, tiled=True)]
    pallas_call x0 -> x2, Pallas kernels: none -> 27.9 us  [the longest x1 17.5 us: exchange(): pl.pallas_call(functools.partial(exchange_kernel, nx, ny), out_shape=(hal...]
    all_to_all x2 -> x0, starting transfers between devices: 10.7 us -> none  [the longest x1 5.4 us: per_device(): lax.all_to_all(deriv, 'gx', split_axis=1, concat_axis=0, tiled=True)]
    add x1 -> x0, other arithmetic: 9.62 us -> none  [per_device(): rhs = -velocity * dudx + forcing[:, None, None] * velocity]
    reshape x1 -> x0, local copies, waits for them, and re-layouts: 8.24 us -> none  [derivative_lines(): inner = full.reshape(own, rows_p - 1, cols_q)]
  transfers between devices with their start and end apart: 2 -> 0, of which waited for: 1 -> 0; matrix products, arithmetic and copies ran while one was open for 1% -> 0% of each run, Pallas kernels for 0% -> 0%
where the time goes in v1:
time: 32.5 us; the launch traced here: 32.2 us
  Pallas kernels  27.9 us (86%)
  local copies, waits for them, and re-layouts  3.68 us (11%)
  between operations  0.65 us (2%)
    pallas_call x1, Pallas kernels, exchange(): pl.pallas_call(functools.partial(exchange_kernel, nx, ny), out_shape=(hal...  17.5 us
    pallas_call x1, Pallas kernels, apply_filter(): pl.pallas_call(functools.partial(filter_kernel, count), grid=(planes // g...  10.4 us
    unnamed x8, local copies, waits for them, and re-layouts  3.68 us

profile of v1, /device:TPU:0, one launch (start us, length us, event | category | flops | bytes accessed | tf_op | source)
XLA Modules:
  0.0 32.2 jit_solution(3477056119931566058)
XLA Ops:
  0.6 0.8 %copy.8.bl_ref = f32[128,10]{1,0:T(8,128)S(1)} copy(f32[128,10]{0,1:T(8,128)} %param.7) | data formatting | bytes 10240 | tf_op args[1]
  1.4 0.8 %copy.9.br_ref = f32[128,10]{1,0:T(8,128)S(1)} copy(f32[128,10]{0,1:T(8,128)} %param.8) | data formatting | bytes 10240 | tf_op args[2]
  2.2 17.5 %exchange.1 = (f32[16,48,128]{2,1,0:T(8,128)S(1)}, f32[16,48,128]{2,1,0:T(8,128)S(1)}, f32[16,128]{1,0:T(8,128)S(1)}) custom-call(f32[16,48,2048]{2,1,0:T(8,128)} %v_ref.3, f32[128,10]{1,0:T(8,128)S(1)} %copy.8.bl_ref, f32[128,10]{1,0:T(8,128)S(1)} %copy.9.br_ref), custom_call_target="tpu_custom_call" | custom-call | tf_op jit(solution)/shard_map/exchange/pallas_call | solution.py:210
  19.7 0.0 copy-start
  19.7 0.7 %copy-done = f32[16,48,128]{2,1,0:T(8,128)} copy-done((f32[16,48,128]{2,1,0:T(8,128)}, f32[16,48,128]{2,1,0:T(8,128)S(1)}, u32[]{:S(2)}) %copy-start) | copy-done | bytes 393240
  20.4 0.0 copy-start.1
  20.4 0.7 %copy-done.1 = f32[16,48,128]{2,1,0:T(8,128)} copy-done((f32[16,48,128]{2,1,0:T(8,128)}, f32[16,48,128]{2,1,0:T(8,128)S(1)}, u32[]{:S(2)}) %copy-start.1) | copy-done | bytes 393240
  21.2 0.0 copy-start.2
  21.2 0.6 %copy-done.2 = f32[16,128]{1,0:T(8,128)} copy-done((f32[16,128]{1,0:T(8,128)}, f32[16,128]{1,0:T(8,128)S(1)}, u32[]{:S(2)}) %copy-start.2) | copy-done | bytes 8216
  21.8 10.4 %filter.1 = (f32[16,48,2048]{2,1,0:T(8,128)}, f32[16,48,2048]{2,1,0:T(8,128)}) custom-call(f32[16,48,2048]{2,1,0:T(8,128)} %v_ref.3, f32[16,48,128]{2,1,0:T(8,128)} %copy-done, f32[16,48,128]{2,1,0:T(8,128)} %copy-done.1, bf16[512,256]{1,0:T(8,128)(2,1)} %constant.4.clone.high_ref, bf16[512,256]{1,0:T(8,128)(2,1)} %constant.5.clone.low_ref, ...), custom_call_target="tpu_custom_call" | custom-call | tf_op jit(solution)/shard_map/filter/pallas_call | solution.py:311
Async XLA Ops:
  19.7 0.8 %copy-start = (f32[16,48,128]{2,1,0:T(8,128)}, f32[16,48,128]{2,1,0:T(8,128)S(1)}, u32[]{:S(2)}) copy-start(f32[16,48,128]{2,1,0:T(8,128)S(1)} %get-tuple-element.5.left_ref) | copy-start | bytes 1179652
  20.4 0.7 %copy-start.1 = (f32[16,48,128]{2,1,0:T(8,128)}, f32[16,48,128]{2,1,0:T(8,128)S(1)}, u32[]{:S(2)}) copy-start(f32[16,48,128]{2,1,0:T(8,128)S(1)} %get-tuple-element.6.right_ref) | copy-start | bytes 1179652
  21.2 0.6 %copy-start.2 = (f32[16,128]{1,0:T(8,128)}, f32[16,128]{1,0:T(8,128)S(1)}, u32[]{:S(2)}) copy-start(f32[16,128]{1,0:T(8,128)S(1)} %get-tuple-element.7.total_ref) | copy-start | bytes 24580

commit v2 on v1

v2 whole, which is shorter than its diff:
```python
import functools

import jax
import jax.numpy as jnp
import numpy as np
from jax import lax
from jax.experimental import pallas as pl
from jax.experimental.pallas import tpu as pltpu
from jax.sharding import PartitionSpec as P

ALPHA = 36.0
ORDER = 36
BLOCK = 256
PACK = 16
HIGH = lax.Precision.HIGHEST


def taps(period):
    freq = np.arange(period)
    half = period // 2
    signed = np.where(freq < half, freq, freq - period).astype(np.float64)
    factor = 2.0 * np.pi / period * signed * np.exp(-ALPHA * (np.abs(signed) / half) ** ORDER)
    factor[half] = 0.0
    return np.fft.ifft(1j * factor).real


def toeplitz(period, reach):
    kernel = taps(period)
    source = np.arange(BLOCK + 2 * reach)[:, None] - reach
    target = np.arange(BLOCK)[None, :]
    table = kernel[(target - source) % period]
    high = table.astype(np.float32).astype(jnp.bfloat16)
    low = (table - high.astype(np.float64)).astype(np.float32).astype(jnp.bfloat16)
    return high, low


def split(x):
    high = x.astype(jnp.bfloat16)
    return high, (x - high.astype(jnp.float32)).astype(jnp.bfloat16)


def exchange_kernel(
    nx, ny, v_ref, bl_ref, br_ref, table_ref, left_ref, right_ref, total_ref, vbuf, inner_ref,
    ehigh, elow, table, xbuf, ybuf, part, ends, blend,
    load_sem, xsend, xrecv, ysend, yrecv, hsend, hrecv, esend, erecv, tsem,
):
    planes, rows, width = v_ref.shape
    reach = left_ref.shape[2]
    depth = bl_ref.shape[0]
    blocks = width // BLOCK
    group = min(4, planes)
    lines = group * rows
    gx = lax.axis_index("gx")
    gy = lax.axis_index("gy")
    first = gx == 0
    last = gx == nx - 1

    def load(p):
        return pltpu.make_async_copy(v_ref.at[p], vbuf.at[p], load_sem.at[p])

    def start_load(p, carry):
        load(p).start()
        return carry

    lax.fori_loop(0, planes, start_load, 0)
    load_table = pltpu.make_async_copy(table_ref, table, tsem)
    load_table.start()

    barrier = pltpu.get_barrier_semaphore()
    for d in range(1, nx):
        pl.semaphore_signal(barrier, inc=1, device_id={"gx": lax.rem(gx + d, nx)})
    for d in range(1, ny):
        pl.semaphore_signal(barrier, inc=1, device_id={"gy": lax.rem(gy + d, ny)})
    pl.semaphore_wait(barrier, nx + ny - 2)

    to_right = pltpu.make_async_remote_copy(
        src_ref=v_ref.at[:, :, pl.ds(width - reach, reach)],
        dst_ref=left_ref,
        send_sem=hsend.at[0],
        recv_sem=hrecv.at[0],
        device_id={"gx": lax.rem(gx + 1, nx)},
    )
    to_left = pltpu.make_async_remote_copy(
        src_ref=v_ref.at[:, :, pl.ds(0, reach)],
        dst_ref=right_ref,
        send_sem=hsend.at[1],
        recv_sem=hrecv.at[1],
        device_id={"gx": lax.rem(gx + nx - 1, nx)},
    )

    @pl.when(jnp.logical_not(last))
    def _():
        to_right.start()

    @pl.when(jnp.logical_not(first))
    def _():
        to_left.start()

    def plane_sum(p, carry):
        load(p).wait()
        x = vbuf[p]
        s = jnp.sum((x * x).reshape(rows // 8, 8, width), axis=0)
        acc = s[:, 0:128]
        for c in range(1, width // 128):
            acc = acc + s[:, c * 128 : (c + 1) * 128]
        part[pl.ds(p, 1), :] = jnp.sum(acc, axis=0, keepdims=True)
        return carry

    lax.fori_loop(0, planes, plane_sum, 0)

    xcopies = []
    for d in range(1, nx):
        copy = pltpu.make_async_remote_copy(
            src_ref=part,
            dst_ref=xbuf.at[d],
            send_sem=xsend.at[d],
            recv_sem=xrecv.at[d],
            device_id={"gx": lax.rem(gx + d, nx)},
        )
        copy.start()
        xcopies.append(copy)

    sel_row = lax.broadcasted_iota(jnp.int32, (PACK, reach), 0)
    sel_col = lax.broadcasted_iota(jnp.int32, (PACK, reach), 1)

    def pack(lane, offset):
        pick = jnp.where((sel_row < depth) & (sel_col == sel_row + offset), 1.0, 0.0)
        tile = vbuf[:, :, lane : lane + reach].reshape(planes * rows, reach)
        return lax.dot_general(
            pick.astype(jnp.float32), tile, (((1,), (1,)), ((), ())), precision=HIGH
        )

    ends_out = pltpu.make_async_remote_copy(
        src_ref=ends.at[0], dst_ref=ends.at[0], send_sem=esend.at[0],
        recv_sem=erecv.at[0], device_id={"gx": nx - 1},
    )
    ends_back = pltpu.make_async_remote_copy(
        src_ref=ends.at[1], dst_ref=ends.at[1], send_sem=esend.at[1],
        recv_sem=erecv.at[1], device_id={"gx": 0},
    )

    @pl.when(first)
    def _():
        ends[0] = pack(0, 0)
        ends_out.start()

    @pl.when(last)
    def _():
        ends[1] = pack(width - reach, reach - depth)
        ends_back.start()

    ehigh[0:lines, 0:reach] = jnp.zeros((lines, reach), jnp.bfloat16)
    elow[0:lines, 0:reach] = jnp.zeros((lines, reach), jnp.bfloat16)
    tail = (pl.ds(blocks * lines, lines), pl.ds(BLOCK - reach, reach))
    ehigh[tail] = jnp.zeros((lines, reach), jnp.bfloat16)
    elow[tail] = jnp.zeros((lines, reach), jnp.bfloat16)

    def put(c, lane, x):
        high, low = split(x.reshape(lines, x.shape[2]))
        spot = (pl.ds(c * lines, lines), pl.ds(lane, x.shape[2]))
        ehigh[spot] = high
        elow[spot] = low

    def inner(step, carry):
        these = pl.ds(step * group, group)
        put(0, reach, vbuf[these, :, 0 : BLOCK - reach])
        for c in range(1, blocks):
            put(c, 0, vbuf[these, :, c * BLOCK - reach : (c + 1) * BLOCK - reach])
        put(blocks, 0, vbuf[these, :, width - reach : width])
        chunk = min(4, blocks)
        for c0 in range(0, blocks, chunk):
            here = pl.ds(c0 * lines, chunk * lines)
            there = pl.ds((c0 + 1) * lines, chunk * lines)
            h0, h1 = ehigh[here, :], ehigh[there, :]
            wide = jnp.concatenate([h0, h1, elow[here, :], elow[there, :], h0, h1], axis=1)
            res = jnp.dot(wide, table[...], preferred_element_type=jnp.float32)
            res = res.reshape(chunk, group, rows, BLOCK)
            for i in range(chunk):
                lane = (c0 + i) * BLOCK
                inner_ref[these, :, lane : lane + BLOCK] = res[i]
        return carry

    load_table.wait()
    inner(0, 0)

    for copy in xcopies:
        copy.wait()
    mine = part[...]
    for d in range(1, nx):
        mine = mine + xbuf[d]
    ybuf[0] = mine
    ycopies = []
    for d in range(1, ny):
        copy = pltpu.make_async_remote_copy(
            src_ref=ybuf.at[0],
            dst_ref=ybuf.at[d],
            send_sem=ysend.at[d],
            recv_sem=yrecv.at[d],
            device_id={"gy": lax.rem(gy + d, ny)},
        )
        copy.start()
        ycopies.append(copy)

    lax.fori_loop(1, planes // group, inner, 0)

    def continuation(halo_ref):
        blend[...] = jnp.zeros_like(blend)
        blend[0, 0:depth, :] = bl_ref[...]
        blend[1, 0:depth, :] = br_ref[...]
        mixed = lax.dot_general(
            ends[...].reshape(2 * PACK, planes * rows),
            blend[...].reshape(2 * PACK, reach),
            (((0,), (0,)), ((), ())),
            precision=HIGH,
        )
        halo_ref[...] = mixed.reshape(halo_ref.shape)

    @pl.when(first)
    def _():
        ends_out.wait_send()
        ends_back.wait_recv()
        continuation(left_ref)

    @pl.when(last)
    def _():
        ends_back.wait_send()
        ends_out.wait_recv()
        continuation(right_ref)

    for copy in ycopies:
        copy.wait()
    every = ybuf[0]
    for d in range(1, ny):
        every = every + ybuf[d]
    total_ref[...] = every

    @pl.when(jnp.logical_not(last))
    def _():
        to_right.wait_send()
        to_left.wait_recv()

    @pl.when(jnp.logical_not(first))
    def _():
        to_left.wait_send()
        to_right.wait_recv()


def exchange(velocity, blend_left, blend_right, table, nx, ny):
    planes, rows, width = velocity.shape
    reach = blend_left.shape[0]
    group = min(4, planes)
    lines = group * rows
    blocks = width // BLOCK
    halo = jax.ShapeDtypeStruct((planes, rows, reach), jnp.float32)
    whole = jax.ShapeDtypeStruct(velocity.shape, jnp.float32)
    dma = pltpu.SemaphoreType.DMA
    vmem = pl.BlockSpec(memory_space=pltpu.VMEM)
    hbm = pl.BlockSpec(memory_space=pltpu.HBM)
    return pl.pallas_call(
        functools.partial(exchange_kernel, nx, ny),
        out_shape=(halo, halo, jax.ShapeDtypeStruct((planes, 128), jnp.float32), whole, whole),
        in_specs=[hbm, vmem, vmem, hbm],
        out_specs=(vmem, vmem, vmem, vmem, vmem),
        scratch_shapes=[
            pltpu.VMEM(((blocks + 1) * lines, BLOCK), jnp.bfloat16),
            pltpu.VMEM(((blocks + 1) * lines, BLOCK), jnp.bfloat16),
            pltpu.VMEM(table.shape, table.dtype),
            pltpu.VMEM((nx, planes, 128), jnp.float32),
            pltpu.VMEM((ny, planes, 128), jnp.float32),
            pltpu.VMEM((planes, 128), jnp.float32),
            pltpu.VMEM((2, PACK, planes * rows), jnp.float32),
            pltpu.VMEM((2, PACK, reach), jnp.float32),
            dma((planes,)),
            dma((nx,)),
            dma((nx,)),
            dma((ny,)),
            dma((ny,)),
            dma((2,)),
            dma((2,)),
            dma((2,)),
            dma((2,)),
            dma,
        ],
        compiler_params=pltpu.CompilerParams(
            collective_id=0, has_side_effects=True, vmem_limit_bytes=38 * 2**20
        ),
        name="exchange",
    )(velocity, blend_left.T, blend_right.T, table)


def finish_kernel(
    count, left_ref, right_ref, tleft_ref, tright_ref, total_ref, inj_ref, v_ref, inner_ref,
    dudx_ref, rhs_ref,
):
    group, rows, width = dudx_ref.shape
    reach = left_ref.shape[2]
    lines = group * rows
    step = pl.program_id(0)
    these = pl.ds(step * group, group)

    def edge(halo_ref, weight_ref):
        high, low = split(halo_ref[these].reshape(lines, reach))
        wide = jnp.concatenate([high, low, high], axis=1)
        res = jnp.dot(wide, weight_ref[...], preferred_element_type=jnp.float32)
        return res.reshape(group, rows, reach)

    from_left = edge(left_ref, tleft_ref)
    from_right = edge(right_ref, tright_ref)
    for g in range(group):
        p = step * group + g
        energy = jnp.sum(total_ref[pl.ds(p, 1), :], axis=1, keepdims=True) / count
        forcing = inj_ref[p] / energy
        for lane in range(0, width, reach):
            spot = pl.ds(lane, reach)
            d = inner_ref[p, :, spot]
            if lane == 0:
                d = d + from_left[g]
            if lane == width - reach:
                d = d + from_right[g]
            dudx_ref[g, :, spot] = d
            rhs_ref[g, :, spot] = v_ref[p, :, spot] * (forcing - d)


def finish(velocity, inner, left, right, total, injection, tleft, tright, count):
    planes, rows, width = velocity.shape
    group = min(2, planes)
    whole = jax.ShapeDtypeStruct(velocity.shape, jnp.float32)
    vmem = pl.BlockSpec(memory_space=pltpu.VMEM)
    part = pl.BlockSpec((group, rows, width), lambda i: (i, 0, 0))
    return pl.pallas_call(
        functools.partial(finish_kernel, count),
        grid=(planes // group,),
        out_shape=(whole, whole),
        in_specs=[vmem] * 5 + [pl.BlockSpec(memory_space=pltpu.SMEM)] + [vmem] * 2,
        out_specs=(part, part),
        compiler_params=pltpu.CompilerParams(vmem_limit_bytes=32 * 2**20),
        name="finish",
    )(left, right, tleft, tright, total, injection, velocity, inner)


def per_device(nx, ny, velocity, blend_left, blend_right, injection):
    planes, rows, width = velocity.shape
    reach = blend_left.shape[0]
    period = width * nx + reach
    count = width * nx * rows * ny
    high, low = toeplitz(period, reach)
    table = jnp.asarray(np.concatenate([high, high, low], axis=0))
    head, foot = slice(0, reach), slice(BLOCK + reach, None)
    near, far = slice(0, reach), slice(BLOCK - reach, None)
    tleft = jnp.asarray(np.concatenate([high[head, near], high[head, near], low[head, near]]))
    tright = jnp.asarray(np.concatenate([high[foot, far], high[foot, far], low[foot, far]]))
    left, right, total, points, inner = exchange(
        velocity, blend_left, blend_right, table, nx, ny
    )
    return finish(points, inner, left, right, total, injection, tleft, tright, count)


def solution(mesh):
    placed = (P(None, "gy", "gx"), P(), P(), P())
    return jax.shard_map(
        functools.partial(per_device, mesh.shape["gx"], mesh.shape["gy"]),
        mesh=mesh,
        in_specs=placed,
        out_specs=(P(None, "gy", "gx"), P(None, "gy", "gx")),
        check_vma=False,
    )
```

time: 32.5 us -> 29.4 us (0.905)
  Pallas kernels: 27.9 us -> 25.9 us
  local copies, waits for them, and re-layouts: 3.68 us -> 2.54 us
    pallas_call x1, Pallas kernels: 10.4 us -> 6.57 us  [finish(): pl.pallas_call(functools.partial(finish_kernel, count), grid=(planes // g...]
    pallas_call x1, Pallas kernels: 17.5 us -> 19.3 us  [exchange(): pl.pallas_call(functools.partial(exchange_kernel, nx, ny), out_shape=(hal...]
    unnamed x8 -> x12, local copies, waits for them, and re-layouts: 3.68 us -> 2.54 us
where the time goes in v2:
time: 29.4 us; the launch traced here: 29.1 us
  Pallas kernels  25.9 us (88%)
  local copies, waits for them, and re-layouts  2.54 us (9%)
  between operations  0.68 us (2%)
    pallas_call x1, Pallas kernels, exchange(): pl.pallas_call(functools.partial(exchange_kernel, nx, ny), out_shape=(hal...  19.3 us
    pallas_call x1, Pallas kernels, finish(): pl.pallas_call(functools.partial(finish_kernel, count), grid=(planes // g...  6.57 us
    unnamed x12, local copies, waits for them, and re-layouts  2.54 us

profile of v2, /device:TPU:0, one launch (start us, length us, event | category | flops | bytes accessed | tf_op | source)
XLA Modules:
  0.0 29.1 jit_solution(5107818588498865987)
XLA Ops:
  0.6 0.0 copy-start.5
  0.6 0.0 copy-start
  0.7 1.1 %copy-done = bf16[1536,256]{1,0:T(8,128)(2,1)S(1)} copy-done((bf16[1536,256]{1,0:T(8,128)(2,1)S(1)}, bf16[1536,256]{1,0:T(8,128)(2,1)}, u32[]{:S(2)}) %copy-start) | copy-done | bytes 786456
  1.8 0.0 copy-start.3
  1.8 0.7 %copy-done.3 = f32[128,10]{0,1:T(8,128)S(1)} copy-done((f32[128,10]{0,1:T(8,128)S(1)}, f32[128,10]{0,1:T(8,128)}, u32[]{:S(2)}) %copy-start.3) | copy-done | bytes 5144
  2.5 0.0 copy-start.4
  2.5 0.7 %copy-done.4 = f32[128,10]{0,1:T(8,128)S(1)} copy-done((f32[128,10]{0,1:T(8,128)S(1)}, f32[128,10]{0,1:T(8,128)}, u32[]{:S(2)}) %copy-start.4) | copy-done | bytes 5144
  3.2 0.0 copy-start.1
  3.2 0.0 copy-start.2
  3.2 19.3 %exchange.1 = (f32[16,48,128]{2,1,0:T(8,128)S(1)}, f32[16,48,128]{2,1,0:T(8,128)S(1)}, f32[16,128]{1,0:T(8,128)S(1)}, f32[16,48,2048]{2,1,0:T(8,128)S(1)}, f32[16,48,2048]{2,1,0:T(8,128)S(1)}) custom-call(f32[16,48,2048]{2,1,0:T(8,128)} %v_ref.1, f32[10,128]{1,0:T(8,128)S(1)} %bitcast.2, f32[10,128]{1,0:T(8,128)S(1)} %bitcast.3, bf16[1536,256]{1,0:T(8,128)(2,1)S(1)} %copy-done), custom_call_target="tpu_custom_call" | custom-call | tf_op jit(solution)/shard_map/exchange/pallas_call | solution.py:259
  22.5 0.0 copy-done.5
  22.5 0.0 copy-done.1
  22.5 0.0 copy-done.2
  22.5 6.6 %finish.1 = (f32[16,48,2048]{2,1,0:T(8,128)}, f32[16,48,2048]{2,1,0:T(8,128)}) custom-call(f32[16,48,128]{2,1,0:T(8,128)S(1)} %get-tuple-element.7.left_ref, f32[16,48,128]{2,1,0:T(8,128)S(1)} %get-tuple-element.8.right_ref, bf16[384,128]{1,0:T(8,128)(2,1)S(1)} %copy-done.2, bf16[384,128]{1,0:T(8,128)(2,1)S(1)} %copy-done.1, ...), custom_call_target="tpu_custom_call" | custom-call | tf_op jit(solution)/shard_map/finish/pallas_call | solution.py:330
Async XLA Ops:
  0.6 21.9 %copy-start.5 = (f32[16]{0:T(128)S(1)}, f32[16]{0:T(128)}, u32[]{:S(2)}) copy-start(f32[16]{0:T(128)} %inj_ref.1) | copy-start | bytes 196
  0.6 1.1 %copy-start = (bf16[1536,256]{1,0:T(8,128)(2,1)S(1)}, bf16[1536,256]{1,0:T(8,128)(2,1)}, u32[]{:S(2)}) copy-start(bf16[1536,256]{1,0:T(8,128)(2,1)} %constant.6.clone.table_ref) | copy-start | bytes 2359300
  1.8 0.7 %copy-start.3 = (f32[128,10]{0,1:T(8,128)S(1)}, f32[128,10]{0,1:T(8,128)}, u32[]{:S(2)}) copy-start(f32[128,10]{0,1:T(8,128)} %param.8) | copy-start | bytes 15364
  2.5 0.7 %copy-start.4 = (f32[128,10]{0,1:T(8,128)S(1)}, f32[128,10]{0,1:T(8,128)}, u32[]{:S(2)}) copy-start(f32[128,10]{0,1:T(8,128)} %param.9) | copy-start | bytes 15364
  3.2 19.3 %copy-start.1 = (bf16[384,128]{1,0:T(8,128)(2,1)S(1)}, bf16[384,128]{1,0:T(8,128)(2,1)}, u32[]{:S(2)}) copy-start(bf16[384,128]{1,0:T(8,128)(2,1)} %constant.8.clone.tright_ref) | copy-start | bytes 294916
  3.2 19.3 %copy-start.2 = (bf16[384,128]{1,0:T(8,128)(2,1)S(1)}, bf16[384,128]{1,0:T(8,128)(2,1)}, u32[]{:S(2)}) copy-start(bf16[384,128]{1,0:T(8,128)(2,1)} %constant.7.clone.tleft_ref) | copy-start | bytes 294916

commit v3 on v2

v3 whole, which is shorter than its diff:
```python
import functools

import jax
import jax.numpy as jnp
import numpy as np
from jax import lax
from jax.experimental import pallas as pl
from jax.experimental.pallas import tpu as pltpu
from jax.sharding import PartitionSpec as P

ALPHA = 36.0
ORDER = 36
BLOCK = 256
PACK = 16
HIGH = lax.Precision.HIGHEST


def taps(period):
    freq = np.arange(period)
    half = period // 2
    signed = np.where(freq < half, freq, freq - period).astype(np.float64)
    factor = 2.0 * np.pi / period * signed * np.exp(-ALPHA * (np.abs(signed) / half) ** ORDER)
    factor[half] = 0.0
    return np.fft.ifft(1j * factor).real


def toeplitz(period, reach):
    kernel = taps(period)
    source = np.arange(BLOCK + 2 * reach)[:, None] - reach
    target = np.arange(BLOCK)[None, :]
    table = kernel[(target - source) % period]
    high = table.astype(np.float32).astype(jnp.bfloat16)
    low = (table - high.astype(np.float64)).astype(np.float32).astype(jnp.bfloat16)
    return high, low


def split(x):
    high = x.astype(jnp.bfloat16)
    return high, (x - high.astype(jnp.float32)).astype(jnp.bfloat16)


def exchange_kernel(
    nx, ny, depth, v_ref, table_ref, left_ref, right_ref, ends, total_ref, vbuf, inner_ref,
    ehigh, elow, table, sums, part,
    load_sem, ssend, srecv, hsend, hrecv, esend, erecv, tsem,
):
    planes, rows, width = v_ref.shape
    reach = left_ref.shape[2]
    blocks = width // BLOCK
    group = min(4, planes)
    lines = group * rows
    gx = lax.axis_index("gx")
    gy = lax.axis_index("gy")
    first = gx == 0
    last = gx == nx - 1

    def load(p):
        return pltpu.make_async_copy(v_ref.at[p], vbuf.at[p], load_sem.at[p])

    def start_load(p, carry):
        load(p).start()
        return carry

    lax.fori_loop(0, planes, start_load, 0)
    deep = BLOCK + 2 * reach
    table_loads = [
        pltpu.make_async_copy(
            table_ref.at[pl.ds(source * deep, deep), :],
            table.at[pl.ds(i * deep, deep), :],
            tsem.at[i],
        )
        for i, source in enumerate((0, 0, 1))
    ]
    for copy in table_loads:
        copy.start()

    barrier = pltpu.get_barrier_semaphore()

    def partner(d):
        return {
            "gx": lax.rem(gx + d // ny, nx),
            "gy": lax.rem(gy + lax.rem(d, ny), ny),
        }

    def greet(d, carry):
        pl.semaphore_signal(barrier, inc=1, device_id=partner(d))
        return carry

    lax.fori_loop(1, nx * ny, greet, 0)
    pl.semaphore_wait(barrier, nx * ny - 1)

    to_right = pltpu.make_async_remote_copy(
        src_ref=v_ref.at[:, :, pl.ds(width - reach, reach)],
        dst_ref=left_ref,
        send_sem=hsend.at[0],
        recv_sem=hrecv.at[0],
        device_id={"gx": lax.rem(gx + 1, nx)},
    )
    to_left = pltpu.make_async_remote_copy(
        src_ref=v_ref.at[:, :, pl.ds(0, reach)],
        dst_ref=right_ref,
        send_sem=hsend.at[1],
        recv_sem=hrecv.at[1],
        device_id={"gx": lax.rem(gx + nx - 1, nx)},
    )

    @pl.when(jnp.logical_not(last))
    def _():
        to_right.start()

    @pl.when(jnp.logical_not(first))
    def _():
        to_left.start()

    def plane_sum(p, carry):
        load(p).wait()
        x = vbuf[p]
        s = jnp.sum((x * x).reshape(rows // 8, 8, width), axis=0)
        acc = s[:, 0:128]
        for c in range(1, width // 128):
            acc = acc + s[:, c * 128 : (c + 1) * 128]
        part[pl.ds(p, 1), :] = jnp.sum(acc, axis=0, keepdims=True)
        return carry

    lax.fori_loop(0, planes, plane_sum, 0)

    row = lax.dot_general(
        jnp.ones((8, 128), jnp.float32), part[...], (((1,), (1,)), ((), ())), precision=HIGH
    )
    sums[0] = jnp.zeros((1, 128), jnp.float32)
    sums[0, :, 0:planes] = row[0:1]

    def give(d, carry):
        pltpu.make_async_remote_copy(
            src_ref=sums.at[0],
            dst_ref=sums.at[d],
            send_sem=ssend,
            recv_sem=srecv,
            device_id=partner(d),
        ).start()
        return carry

    lax.fori_loop(1, nx * ny, give, 0)

    sel_row = lax.broadcasted_iota(jnp.int32, (PACK, reach), 0)
    sel_col = lax.broadcasted_iota(jnp.int32, (PACK, reach), 1)

    def pack(lane, offset):
        pick = jnp.where((sel_row < depth) & (sel_col == sel_row + offset), 1.0, 0.0)
        tile = vbuf[:, :, lane : lane + reach].reshape(planes * rows, reach)
        return lax.dot_general(
            pick.astype(jnp.float32), tile, (((1,), (1,)), ((), ())), precision=HIGH
        )

    ends_out = pltpu.make_async_remote_copy(
        src_ref=ends.at[0], dst_ref=ends.at[0], send_sem=esend.at[0],
        recv_sem=erecv.at[0], device_id={"gx": nx - 1},
    )
    ends_back = pltpu.make_async_remote_copy(
        src_ref=ends.at[1], dst_ref=ends.at[1], send_sem=esend.at[1],
        recv_sem=erecv.at[1], device_id={"gx": 0},
    )

    @pl.when(first)
    def _():
        ends[0] = pack(0, 0)
        ends_out.start()

    @pl.when(last)
    def _():
        ends[1] = pack(width - reach, reach - depth)
        ends_back.start()

    ehigh[0:lines, 0:reach] = jnp.zeros((lines, reach), jnp.bfloat16)
    elow[0:lines, 0:reach] = jnp.zeros((lines, reach), jnp.bfloat16)
    tail = (pl.ds(blocks * lines, lines), pl.ds(BLOCK - reach, reach))
    ehigh[tail] = jnp.zeros((lines, reach), jnp.bfloat16)
    elow[tail] = jnp.zeros((lines, reach), jnp.bfloat16)

    def put(c, lane, x):
        high, low = split(x.reshape(lines, x.shape[2]))
        spot = (pl.ds(c * lines, lines), pl.ds(lane, x.shape[2]))
        ehigh[spot] = high
        elow[spot] = low

    def inner(step, carry):
        these = pl.ds(step * group, group)
        put(0, reach, vbuf[these, :, 0 : BLOCK - reach])
        for c in range(1, blocks):
            put(c, 0, vbuf[these, :, c * BLOCK - reach : (c + 1) * BLOCK - reach])
        put(blocks, 0, vbuf[these, :, width - reach : width])
        chunk = min(4, blocks)
        for c0 in range(0, blocks, chunk):
            here = pl.ds(c0 * lines, chunk * lines)
            there = pl.ds((c0 + 1) * lines, chunk * lines)
            h0, h1 = ehigh[here, :], ehigh[there, :]
            wide = jnp.concatenate([h0, h1, elow[here, :], elow[there, :], h0, h1], axis=1)
            res = jnp.dot(wide, table[...], preferred_element_type=jnp.float32)
            res = res.reshape(chunk, group, rows, BLOCK)
            for i in range(chunk):
                lane = (c0 + i) * BLOCK
                inner_ref[these, :, lane : lane + BLOCK] = res[i]
        return carry

    for copy in table_loads:
        copy.wait()
    lax.fori_loop(0, planes // group, inner, 0)

    @pl.when(first)
    def _():
        ends_out.wait_send()
        ends_back.wait_recv()

    @pl.when(last)
    def _():
        ends_back.wait_send()
        ends_out.wait_recv()

    others = sums.at[pl.ds(1, nx * ny - 1)]
    pltpu.make_async_copy(others, others, ssend).wait()
    pltpu.make_async_copy(others, others, srecv).wait()
    total_ref[...] = jnp.sum(sums[...], axis=0)

    @pl.when(jnp.logical_not(last))
    def _():
        to_right.wait_send()
        to_left.wait_recv()

    @pl.when(jnp.logical_not(first))
    def _():
        to_left.wait_send()
        to_right.wait_recv()


def exchange(velocity, table, reach, depth, nx, ny):
    planes, rows, width = velocity.shape
    group = min(4, planes)
    lines = group * rows
    blocks = width // BLOCK
    halo = jax.ShapeDtypeStruct((planes, rows, reach), jnp.float32)
    ends = jax.ShapeDtypeStruct((2, PACK, planes * rows), jnp.float32)
    total = jax.ShapeDtypeStruct((1, 128), jnp.float32)
    whole = jax.ShapeDtypeStruct(velocity.shape, jnp.float32)
    dma = pltpu.SemaphoreType.DMA
    vmem = pl.BlockSpec(memory_space=pltpu.VMEM)
    hbm = pl.BlockSpec(memory_space=pltpu.HBM)
    return pl.pallas_call(
        functools.partial(exchange_kernel, nx, ny, depth),
        out_shape=(halo, halo, ends, total, whole, whole),
        in_specs=[hbm, hbm],
        out_specs=(vmem,) * 6,
        scratch_shapes=[
            pltpu.VMEM(((blocks + 1) * lines, BLOCK), jnp.bfloat16),
            pltpu.VMEM(((blocks + 1) * lines, BLOCK), jnp.bfloat16),
            pltpu.VMEM((3 * (BLOCK + 2 * reach), BLOCK), table.dtype),
            pltpu.VMEM((nx * ny, 1, 128), jnp.float32),
            pltpu.VMEM((planes, 128), jnp.float32),
            dma((planes,)),
            dma,
            dma,
            dma((2,)),
            dma((2,)),
            dma((2,)),
            dma((2,)),
            dma((3,)),
        ],
        compiler_params=pltpu.CompilerParams(
            collective_id=0, has_side_effects=True, vmem_limit_bytes=38 * 2**20
        ),
        name="exchange",
    )(velocity, table)


def finish_kernel(
    nx, count, left_ref, right_ref, ends_ref, bl_ref, br_ref, tleft_ref, tright_ref,
    total_ref, inj_ref, v_ref, inner_ref, dudx_ref, rhs_ref,
    halo, blend, near, far, rbuf, isem, nsem, rsem,
):
    planes, rows, width = v_ref.shape
    reach = left_ref.shape[2]
    depth = bl_ref.shape[0]
    lines = planes * rows
    gx = lax.axis_index("gx")
    middle = pl.ds(reach, width - 2 * reach)

    def inside(p):
        return pltpu.make_async_copy(
            inner_ref.at[p, :, middle], dudx_ref.at[p, :, middle], isem.at[p]
        )

    for p in range(planes):
        inside(p).start()

    def continuation():
        blend[...] = jnp.zeros_like(blend)
        blend[0, 0:depth, :] = bl_ref[...]
        blend[1, 0:depth, :] = br_ref[...]
        return lax.dot_general(
            ends_ref[...].reshape(2 * PACK, lines),
            blend[...].reshape(2 * PACK, reach),
            (((0,), (0,)), ((), ())),
            precision=HIGH,
        )

    def edge(halo_ref, own, weight_ref, lane, result):
        @pl.when(own)
        def _():
            halo[...] = continuation()

        @pl.when(jnp.logical_not(own))
        def _():
            halo[...] = halo_ref[...].reshape(lines, reach)

        high, low = split(halo[...])
        wide = jnp.concatenate([high, low, high], axis=1)
        res = jnp.dot(wide, weight_ref[...], preferred_element_type=jnp.float32)
        result[...] = inner_ref[:, :, lane : lane + reach] + res.reshape(planes, rows, reach)

    edge(left_ref, gx == 0, tleft_ref, 0, near)
    put_near = pltpu.make_async_copy(near, dudx_ref.at[:, :, pl.ds(0, reach)], nsem.at[0])
    put_near.start()
    edge(right_ref, gx == nx - 1, tright_ref, width - reach, far)
    put_far = pltpu.make_async_copy(
        far, dudx_ref.at[:, :, pl.ds(width - reach, reach)], nsem.at[1]
    )
    put_far.start()

    place = lax.broadcasted_iota(jnp.int32, (1, 128), 1)
    total = total_ref[...]

    def put_rhs(p):
        return pltpu.make_async_copy(rbuf.at[p], rhs_ref.at[p], rsem.at[p])

    def plane(p, carry):
        here = jnp.sum(jnp.where(place == p, total, 0.0), axis=1, keepdims=True)
        forcing = inj_ref[p] / (here / count)
        low, high = pl.ds(0, reach), pl.ds(width - reach, reach)
        rbuf[p, :, low] = v_ref[p, :, low] * (forcing - near[p])
        rbuf[p, :, middle] = v_ref[p, :, middle] * (forcing - inner_ref[p, :, middle])
        rbuf[p, :, high] = v_ref[p, :, high] * (forcing - far[p])
        put_rhs(p).start()
        return carry

    lax.fori_loop(0, planes, plane, 0)
    for p in range(planes):
        inside(p).wait()
    put_near.wait()
    put_far.wait()
    for p in range(planes):
        put_rhs(p).wait()


def finish(nx, count, velocity, inner, left, right, ends, blends, total, injection, tables):
    planes, rows, width = velocity.shape
    reach = left.shape[2]
    whole = jax.ShapeDtypeStruct(velocity.shape, jnp.float32)
    vmem = pl.BlockSpec(memory_space=pltpu.VMEM)
    hbm = pl.BlockSpec(memory_space=pltpu.HBM)
    dma = pltpu.SemaphoreType.DMA
    strip = pltpu.VMEM((planes, rows, reach), jnp.float32)
    return pl.pallas_call(
        functools.partial(finish_kernel, nx, count),
        out_shape=(whole, whole),
        in_specs=[vmem] * 8 + [pl.BlockSpec(memory_space=pltpu.SMEM)] + [vmem] * 2,
        out_specs=(hbm, hbm),
        scratch_shapes=[
            pltpu.VMEM((planes * rows, reach), jnp.float32),
            pltpu.VMEM((2, PACK, reach), jnp.float32),
            strip,
            strip,
            pltpu.VMEM(velocity.shape, jnp.float32),
            dma((planes,)),
            dma((2,)),
            dma((planes,)),
        ],
        compiler_params=pltpu.CompilerParams(vmem_limit_bytes=36 * 2**20),
        name="finish",
    )(left, right, ends, *blends, *tables, total, injection, velocity, inner)


def per_device(nx, ny, velocity, blend_left, blend_right, injection):
    planes, rows, width = velocity.shape
    reach = blend_left.shape[0]
    period = width * nx + reach
    count = width * nx * rows * ny
    high, low = toeplitz(period, reach)
    table = jnp.asarray(np.concatenate([high, low], axis=0))
    head, foot = slice(0, reach), slice(BLOCK + reach, None)
    near, far = slice(0, reach), slice(BLOCK - reach, None)
    tleft = jnp.asarray(np.concatenate([high[head, near], high[head, near], low[head, near]]))
    tright = jnp.asarray(np.concatenate([high[foot, far], high[foot, far], low[foot, far]]))
    left, right, ends, total, points, inner = exchange(
        velocity, table, reach, blend_left.shape[1], nx, ny
    )
    blends = (blend_left.T, blend_right.T)
    return finish(
        nx, count, points, inner, left, right, ends, blends, total, injection, (tleft, tright)
    )


def solution(mesh):
    placed = (P(None, "gy", "gx"), P(), P(), P())
    return jax.shard_map(
        functools.partial(per_device, mesh.shape["gx"], mesh.shape["gy"]),
        mesh=mesh,
        in_specs=placed,
        out_specs=(P(None, "gy", "gx"), P(None, "gy", "gx")),
        check_vma=False,
    )
```

time: 29.4 us -> 22.5 us (0.77)
  Pallas kernels: 25.9 us -> 20.6 us
  local copies, waits for them, and re-layouts: 2.54 us -> 1.06 us
    pallas_call x2, Pallas kernels: 25.9 us -> 20.6 us  [the longest x1 15.2 us: exchange(): pl.pallas_call(functools.partial(exchange_kernel, nx, ny, depth), out_sha...]
    unnamed x12, local copies, waits for them, and re-layouts: 2.54 us -> 1.06 us
where the time goes in v3:
time: 22.5 us; the launch traced here: 22.4 us
  Pallas kernels  20.6 us (92%)
  local copies, waits for them, and re-layouts  1.06 us (5%)
  between operations  0.7 us (3%)
    pallas_call x1, Pallas kernels, exchange(): pl.pallas_call(functools.partial(exchange_kernel, nx, ny, depth), out_sha...  15.2 us
    pallas_call x1, Pallas kernels, finish(): pl.pallas_call(functools.partial(finish_kernel, nx, count), out_shape=(wh...  5.38 us
    unnamed x12, local copies, waits for them, and re-layouts  1.06 us

profile of v3, /device:TPU:0, one launch (start us, length us, event | category | flops | bytes accessed | tf_op | source)
XLA Modules:
  0.0 22.4 jit_solution(2531433310991800749)
XLA Ops:
  0.6 0.0 copy-start.5
  0.6 0.0 copy-start
  0.7 1.0 %copy-done = bf16[1024,256]{1,0:T(8,128)(2,1)S(1)} copy-done((bf16[1024,256]{1,0:T(8,128)(2,1)S(1)}, bf16[1024,256]{1,0:T(8,128)(2,1)}, u32[]{:S(2)}) %copy-start) | copy-done | bytes 524312
  1.7 0.0 copy-start.1
  1.7 0.0 copy-start.2
  1.7 0.0 copy-start.3
  1.7 0.0 copy-start.4
  1.7 15.2 %exchange.1 = (f32[16,48,128]{2,1,0:T(8,128)S(1)}, f32[16,48,128]{2,1,0:T(8,128)S(1)}, f32[2,16,768]{2,1,0:T(8,128)S(1)}, f32[1,128]{1,0:T(1,128)S(1)}, f32[16,4...) custom-call(f32[16,48,2048]{2,1,0:T(8,128)} %v_ref.1, bf16[1024,256]{1,0:T(8,128)(2,1)S(1)} %copy-done), custom_call_target="tpu_custom_call" | custom-call | tf_op jit(solution)/shard_map/exchange/pallas_call | solution.py:247
  16.9 0.0 copy-done.5
  16.9 0.0 copy-done.1
  17.0 0.0 copy-done.2
  17.0 0.0 copy-done.3
  17.0 0.0 copy-done.4
  17.0 5.4 %finish.1 = (f32[16,48,2048]{2,1,0:T(8,128)}, f32[16,48,2048]{2,1,0:T(8,128)}) custom-call(f32[16,48,128]{2,1,0:T(8,128)S(1)} %get-tuple-element.8.left_ref, f32[16,48,128]{2,1,0:T(8,128)S(1)} %get-tuple-element.9.right_ref, f32[2,16,768]{2,1,0:T(8,128)S(1)} %get-tuple-element.10.ends_ref, f32[10,128]{1,0:T(8,128)S(1)} %bitcast.2, f32[10,128]{1,0:T(8,128)S(1)} %bitcast.3, ...), custom_call_target="tpu_custom_call" | custom-call | tf_op jit(solution)/shard_map/finish/pallas_call | solution.py:361
Async XLA Ops:
  0.6 16.3 %copy-start.5 = (f32[16]{0:T(128)S(1)}, f32[16]{0:T(128)}, u32[]{:S(2)}) copy-start(f32[16]{0:T(128)} %inj_ref.1) | copy-start | bytes 196
  0.6 1.0 %copy-start = (bf16[1024,256]{1,0:T(8,128)(2,1)S(1)}, bf16[1024,256]{1,0:T(8,128)(2,1)}, u32[]{:S(2)}) copy-start(bf16[1024,256]{1,0:T(8,128)(2,1)} %constant.6.clone.table_ref) | copy-start | bytes 1572868
  1.7 15.3 %copy-start.1 = (bf16[384,128]{1,0:T(8,128)(2,1)S(1)}, bf16[384,128]{1,0:T(8,128)(2,1)}, u32[]{:S(2)}) copy-start(bf16[384,128]{1,0:T(8,128)(2,1)} %constant.8.clone.tright_ref) | copy-start | bytes 294916
  1.7 15.3 %copy-start.2 = (bf16[384,128]{1,0:T(8,128)(2,1)S(1)}, bf16[384,128]{1,0:T(8,128)(2,1)}, u32[]{:S(2)}) copy-start(bf16[384,128]{1,0:T(8,128)(2,1)} %constant.7.clone.tleft_ref) | copy-start | bytes 294916
  1.7 15.3 %copy-start.3 = (f32[128,10]{0,1:T(8,128)S(1)}, f32[128,10]{0,1:T(8,128)}, u32[]{:S(2)}) copy-start(f32[128,10]{0,1:T(8,128)} %param.8) | copy-start | bytes 15364
  1.7 15.3 %copy-start.4 = (f32[128,10]{0,1:T(8,128)S(1)}, f32[128,10]{0,1:T(8,128)}, u32[]{:S(2)}) copy-start(f32[128,10]{0,1:T(8,128)} %param.9) | copy-start | bytes 15364

commit v4 on v3

--- a/solution.py
+++ b/solution.py
@@ -87,90 +87,6 @@
         return carry
 
     lax.fori_loop(1, nx * ny, greet, 0)
-    pl.semaphore_wait(barrier, nx * ny - 1)
-
-    to_right = pltpu.make_async_remote_copy(
-        src_ref=v_ref.at[:, :, pl.ds(width - reach, reach)],
-        dst_ref=left_ref,
-        send_sem=hsend.at[0],
-        recv_sem=hrecv.at[0],
-        device_id={"gx": lax.rem(gx + 1, nx)},
-    )
-    to_left = pltpu.make_async_remote_copy(
-        src_ref=v_ref.at[:, :, pl.ds(0, reach)],
-        dst_ref=right_ref,
-        send_sem=hsend.at[1],
-        recv_sem=hrecv.at[1],
-        device_id={"gx": lax.rem(gx + nx - 1, nx)},
-    )
-
-    @pl.when(jnp.logical_not(last))
-    def _():
-        to_right.start()
-
-    @pl.when(jnp.logical_not(first))
-    def _():
-        to_left.start()
-
-    def plane_sum(p, carry):
-        load(p).wait()
-        x = vbuf[p]
-        s = jnp.sum((x * x).reshape(rows // 8, 8, width), axis=0)
-        acc = s[:, 0:128]
-        for c in range(1, width // 128):
-            acc = acc + s[:, c * 128 : (c + 1) * 128]
-        part[pl.ds(p, 1), :] = jnp.sum(acc, axis=0, keepdims=True)
-        return carry
-
-    lax.fori_loop(0, planes, plane_sum, 0)
-
-    row = lax.dot_general(
-        jnp.ones((8, 128), jnp.float32), part[...], (((1,), (1,)), ((), ())), precision=HIGH
-    )
-    sums[0] = jnp.zeros((1, 128), jnp.float32)
-    sums[0, :, 0:planes] = row[0:1]
-
-    def give(d, carry):
-        pltpu.make_async_remote_copy(
-            src_ref=sums.at[0],
-            dst_ref=sums.at[d],
-            send_sem=ssend,
-            recv_sem=srecv,
-            device_id=partner(d),
-        ).start()
-        return carry
-
-    lax.fori_loop(1, nx * ny, give, 0)
-
-    sel_row = lax.broadcasted_iota(jnp.int32, (PACK, reach), 0)
-    sel_col = lax.broadcasted_iota(jnp.int32, (PACK, reach), 1)
-
-    def pack(lane, offset):
-        pick = jnp.where((sel_row < depth) & (sel_col == sel_row + offset), 1.0, 0.0)
-        tile = vbuf[:, :, lane : lane + reach].reshape(planes * rows, reach)
-        return lax.dot_general(
-            pick.astype(jnp.float32), tile, (((1,), (1,)), ((), ())), precision=HIGH
-        )
-
-    ends_out = pltpu.make_async_remote_copy(
-        src_ref=ends.at[0], dst_ref=ends.at[0], send_sem=esend.at[0],
-        recv_sem=erecv.at[0], device_id={"gx": nx - 1},
-    )
-    ends_back = pltpu.make_async_remote_copy(
-        src_ref=ends.at[1], dst_ref=ends.at[1], send_sem=esend.at[1],
-        recv_sem=erecv.at[1], device_id={"gx": 0},
-    )
-
-    @pl.when(first)
-    def _():
-        ends[0] = pack(0, 0)
-        ends_out.start()
-
-    @pl.when(last)
-    def _():
-        ends[1] = pack(width - reach, reach - depth)
-        ends_back.start()
-
     ehigh[0:lines, 0:reach] = jnp.zeros((lines, reach), jnp.bfloat16)
     elow[0:lines, 0:reach] = jnp.zeros((lines, reach), jnp.bfloat16)
     tail = (pl.ds(blocks * lines, lines), pl.ds(BLOCK - reach, reach))
@@ -202,9 +118,100 @@
                 inner_ref[these, :, lane : lane + BLOCK] = res[i]
         return carry
 
+    def finish_load(p, carry):
+        load(p).wait()
+        return carry
+
     for copy in table_loads:
         copy.wait()
-    lax.fori_loop(0, planes // group, inner, 0)
+    lax.fori_loop(0, group, finish_load, 0)
+    inner(0, 0)
+    lax.fori_loop(group, planes, finish_load, 0)
+
+    def plane_sum(p, carry):
+        x = vbuf[p]
+        s = jnp.sum((x * x).reshape(rows // 8, 8, width), axis=0)
+        acc = s[:, 0:128]
+        for c in range(1, width // 128):
+            acc = acc + s[:, c * 128 : (c + 1) * 128]
+        part[pl.ds(p, 1), :] = jnp.sum(acc, axis=0, keepdims=True)
+        return carry
+
+    lax.fori_loop(0, planes, plane_sum, 0)
+
+    row = lax.dot_general(
+        jnp.ones((8, 128), jnp.float32), part[...], (((1,), (1,)), ((), ())), precision=HIGH
+    )
+    sums[0] = jnp.zeros((1, 128), jnp.float32)
+    sums[0, :, 0:planes] = row[0:1]
+
+    pl.semaphore_wait(barrier, nx * ny - 1)
+
+    to_right = pltpu.make_async_remote_copy(
+        src_ref=v_ref.at[:, :, pl.ds(width - reach, reach)],
+        dst_ref=left_ref,
+        send_sem=hsend.at[0],
+        recv_sem=hrecv.at[0],
+        device_id={"gx": lax.rem(gx + 1, nx)},
+    )
+    to_left = pltpu.make_async_remote_copy(
+        src_ref=v_ref.at[:, :, pl.ds(0, reach)],
+        dst_ref=right_ref,
+        send_sem=hsend.at[1],
+        recv_sem=hrecv.at[1],
+        device_id={"gx": lax.rem(gx + nx - 1, nx)},
+    )
+
+    def give(d, carry):
+        pltpu.make_async_remote_copy(
+            src_ref=sums.at[0],
+            dst_ref=sums.at[d],
+            send_sem=ssend,
+            recv_sem=srecv,
+            device_id=partner(d),
+        ).start()
+        return carry
+
+    lax.fori_loop(1, nx * ny, give, 0)
+
+    @pl.when(jnp.logical_not(last))
+    def _():
+        to_right.start()
+
+    @pl.when(jnp.logical_not(first))
+    def _():
+        to_left.start()
+
+    sel_row = lax.broadcasted_iota(jnp.int32, (PACK, reach), 0)
+    sel_col = lax.broadcasted_iota(jnp.int32, (PACK, reach), 1)
+
+    def pack(lane, offset):
+        pick = jnp.where((sel_row < depth) & (sel_col == sel_row + offset), 1.0, 0.0)
+        tile = vbuf[:, :, lane : lane + reach].reshape(planes * rows, reach)
+        return lax.dot_general(
+            pick.astype(jnp.float32), tile, (((1,), (1,)), ((), ())), precision=HIGH
+        )
+
+    ends_out = pltpu.make_async_remote_copy(
+        src_ref=ends.at[0], dst_ref=ends.at[0], send_sem=esend.at[0],
+        recv_sem=erecv.at[0], device_id={"gx": nx - 1},
+    )
+    ends_back = pltpu.make_async_remote_copy(
+        src_ref=ends.at[1], dst_ref=ends.at[1], send_sem=esend.at[1],
+        recv_sem=erecv.at[1], device_id={"gx": 0},
+    )
+
+    @pl.when(first)
+    def _():
+        ends[0] = pack(0, 0)
+        ends_out.start()
+
+    @pl.when(last)
+    def _():
+        ends[1] = pack(width - reach, reach - depth)
+        ends_back.start()
+
+    lax.fori_loop(1, planes // group, inner, 0)
 
     @pl.when(first)
     def _():

time: 22.5 us -> 21.6 us (0.960)
  the two profiles are of different devices: /device:TPU:0 before, /device:TPU:1 now
where the time goes in v4:
time: 21.6 us; the launch traced here: 21.4 us
  Pallas kernels  19.7 us (91%)
  local copies, waits for them, and re-layouts  1.06 us (5%)
  between operations  0.7 us (3%)
    pallas_call x1, Pallas kernels, exchange(): pl.pallas_call(functools.partial(exchange_kernel, nx, ny, depth), out_sha...  14.3 us
    pallas_call x1, Pallas kernels, finish(): pl.pallas_call(functools.partial(finish_kernel, nx, count), out_shape=(wh...  5.38 us
    unnamed x12, local copies, waits for them, and re-layouts  1.06 us

profile of v4, /device:TPU:1, one launch (start us, length us, event | category | flops | bytes accessed | tf_op | source)
XLA Modules:
  0.0 21.4 jit_solution(9642964570848460306)
XLA Ops:
  0.6 0.0 copy-start.5
  0.6 0.0 copy-start
  0.7 1.0 %copy-done = bf16[1024,256]{1,0:T(8,128)(2,1)S(1)} copy-done((bf16[1024,256]{1,0:T(8,128)(2,1)S(1)}, bf16[1024,256]{1,0:T(8,128)(2,1)}, u32[]{:S(2)}) %copy-start) | copy-done | bytes 524312
  1.7 0.0 copy-start.1
  1.7 0.0 copy-start.2
  1.7 0.0 copy-start.3
  1.7 0.0 copy-start.4
  1.7 14.3 %exchange.1 = (f32[16,48,128]{2,1,0:T(8,128)S(1)}, f32[16,48,128]{2,1,0:T(8,128)S(1)}, f32[2,16,768]{2,1,0:T(8,128)S(1)}, f32[1,128]{1,0:T(1,128)S(1)}, f32[16,4...) custom-call(f32[16,48,2048]{2,1,0:T(8,128)} %v_ref.1, bf16[1024,256]{1,0:T(8,128)(2,1)S(1)} %copy-done), custom_call_target="tpu_custom_call" | custom-call | tf_op jit(solution)/shard_map/exchange/pallas_call | solution.py:254
  16.0 0.0 copy-done.5
  16.0 0.0 copy-done.1
  16.0 0.0 copy-done.2
  16.0 0.0 copy-done.3
  16.0 0.0 copy-done.4
  16.1 5.4 %finish.1 = (f32[16,48,2048]{2,1,0:T(8,128)}, f32[16,48,2048]{2,1,0:T(8,128)}) custom-call(f32[16,48,128]{2,1,0:T(8,128)S(1)} %get-tuple-element.8.left_ref, f32[16,48,128]{2,1,0:T(8,128)S(1)} %get-tuple-element.9.right_ref, f32[2,16,768]{2,1,0:T(8,128)S(1)} %get-tuple-element.10.ends_ref, f32[10,128]{1,0:T(8,128)S(1)} %bitcast.2, f32[10,128]{1,0:T(8,128)S(1)} %bitcast.3, ...), custom_call_target="tpu_custom_call" | custom-call | tf_op jit(solution)/shard_map/finish/pallas_call | solution.py:368
Async XLA Ops:
  0.6 15.4 %copy-start.5 = (f32[16]{0:T(128)S(1)}, f32[16]{0:T(128)}, u32[]{:S(2)}) copy-start(f32[16]{0:T(128)} %inj_ref.1) | copy-start | bytes 196
  0.6 1.0 %copy-start = (bf16[1024,256]{1,0:T(8,128)(2,1)S(1)}, bf16[1024,256]{1,0:T(8,128)(2,1)}, u32[]{:S(2)}) copy-start(bf16[1024,256]{1,0:T(8,128)(2,1)} %constant.6.clone.table_ref) | copy-start | bytes 1572868
  1.7 14.3 %copy-start.1 = (bf16[384,128]{1,0:T(8,128)(2,1)S(1)}, bf16[384,128]{1,0:T(8,128)(2,1)}, u32[]{:S(2)}) copy-start(bf16[384,128]{1,0:T(8,128)(2,1)} %constant.8.clone.tright_ref) | copy-start | bytes 294916
  1.7 14.3 %copy-start.2 = (bf16[384,128]{1,0:T(8,128)(2,1)S(1)}, bf16[384,128]{1,0:T(8,128)(2,1)}, u32[]{:S(2)}) copy-start(bf16[384,128]{1,0:T(8,128)(2,1)} %constant.7.clone.tleft_ref) | copy-start | bytes 294916
  1.7 14.3 %copy-start.3 = (f32[128,10]{0,1:T(8,128)S(1)}, f32[128,10]{0,1:T(8,128)}, u32[]{:S(2)}) copy-start(f32[128,10]{0,1:T(8,128)} %param.8) | copy-start | bytes 15364
  1.7 14.3 %copy-start.4 = (f32[128,10]{0,1:T(8,128)S(1)}, f32[128,10]{0,1:T(8,128)}, u32[]{:S(2)}) copy-start(f32[128,10]{0,1:T(8,128)} %param.9) | copy-start | bytes 15364
